TPU v7x, 32 devices: a whole 2x2x4 slice. The times are simulated.
32 devices in a mesh: dom: 8 (over z, x), attr: 4 (over y, core).
Axes of the slice: x: 2, y: 2, z: 4, core: 2. Of those that a mesh axis runs over, the one named last changes fastest.
Arguments:
- records: bfloat16 [12288, 1024], P('dom', 'attr'), may hold values from -6 to 6
- owner: int32 [12288, 1], P('dom'), may hold values from 0 to 7; in each aligned block of 1536 rows (0 to 1535, 1536 to 3071, ...) at most 384 rows name the same one
- entity_means: bfloat16 [4096, 1024], P('dom', 'attr'), may hold values from -6 to 6
- noise_bits: int32 [24576, 512], P('dom'), may hold values from 0 to 8191
Outputs:
- new_means: float32 [4096, 1024], P('dom', 'attr')
- gram: float32 [1024, 1024], P(('dom', 'attr'))
Inputs may be any that keep to these rules, and one draw needn't show every extreme that they name: `owner`: among the records of one index of dom at most 384 name the same partition, and in every draw some partition is named by exactly 384 of them.
All inputs are finite; a program needn't handle non-finite values.
Results may differ from a plain program's by a relative error of at most 0.0013.
Values may be sent and summed in bfloat16 or wider, within the bound.
A program may use at most 64 MiB of HBM per device.

v0:
```python
import jax
import jax.numpy as jnp
from jax import lax
from jax.sharding import PartitionSpec as P


def posterior(raw, bits, live, width):
    uniform = (bits.astype(jnp.float32) + 0.5) / 8192.0
    noise = -jnp.log(-jnp.log(uniform))
    logits = 3.0 * jnp.tanh(raw * width ** (-0.5)) + noise
    expd = jnp.exp(logits)
    return (expd / jnp.sum(expd, axis=1, keepdims=True) * live[:, None]).astype(jnp.bfloat16)


def shards(records, owner, entity_means, noise_bits):
    dom_count = lax.axis_size("dom")
    attr_count = lax.axis_size("attr")
    rec_dev, feat_cols = records.shape
    slot_count = 2 * rec_dev
    capacity = slot_count // dom_count
    width = feat_cols * attr_count
    total_records = rec_dev * dom_count
    dest = owner[:, 0]
    onehot = (dest[:, None] == jnp.arange(dom_count, dtype=jnp.int32)[None, :]).astype(jnp.int32)
    rank = jnp.sum(jnp.cumsum(onehot, axis=0) * onehot, axis=1) - 1
    position = dest * capacity + rank
    packed = jnp.zeros((slot_count, feat_cols), jnp.bfloat16).at[position].set(records)
    flag_buf = (
        jnp.zeros((slot_count,), jnp.bfloat16).at[position].set(jnp.ones((rec_dev,), jnp.bfloat16))
    )
    arrived, arrived_flags = (
        lax.all_to_all(
            packed.reshape(dom_count, capacity, feat_cols),
            "dom",
            split_axis=0,
            concat_axis=0,
            tiled=True,
        ),
        lax.all_to_all(
            flag_buf.reshape(dom_count, capacity), "dom", split_axis=0, concat_axis=0, tiled=True
        ),
    )
    arrived = arrived.reshape(slot_count, feat_cols)
    live = arrived_flags.reshape(slot_count).astype(jnp.float32)
    raw = lax.psum(jnp.dot(arrived, entity_means.T, preferred_element_type=jnp.float32), "attr")
    weights = posterior(raw, noise_bits, live, width)
    sums_cols = jnp.dot(weights.T, arrived, preferred_element_type=jnp.float32)
    mass_col = jnp.sum(weights.astype(jnp.float32), axis=0)[:, None]
    recon = jnp.dot(weights, entity_means, preferred_element_type=jnp.float32)
    col_resid = ((arrived.astype(jnp.float32) - recon) * live[:, None]).astype(jnp.bfloat16)
    residual = lax.all_to_all(col_resid, "attr", split_axis=0, concat_axis=1, tiled=True)
    new_means = (sums_cols + 1.0 * entity_means.astype(jnp.float32)) / (mass_col + 1.0)
    term = lax.dot_general(
        residual, residual, (((0,), (0,)), ((), ())), preferred_element_type=jnp.float32
    )
    gram = lax.psum_scatter(term / total_records, ("dom", "attr"), scatter_dimension=0, tiled=True)
    return (new_means, gram)


def solution(mesh):
    in_specs = (P("dom", "attr"), P("dom", None), P("dom", "attr"), P("dom", None))
    out_specs = (P("dom", "attr"), P(("dom", "attr"), None))
    return jax.shard_map(shards, mesh=mesh, in_specs=in_specs, out_specs=out_specs, check_vma=False)
```

profile of v0, /device:TPU:0, one launch (start us, length us, event | category | flops | bytes accessed | tf_op | source)
XLA Modules:
  0.0 378.6 jit_solution(3994553369799011512)
XLA Ops:
  7.2 0.7 reduce
  7.9 2.3 reduce-window.6
  10.2 0.3 slice_reduce_fusion
  10.5 0.2 reduce-window.9
  10.7 0.1 add_bitcast_fusion
  10.8 0.7 fusion.8
  11.6 8.0 %scatter_custom_fusion = bf16[3072,256]{1,0:T(8,128)(2,1)S(1)} fusion(s32[1536]{0:T(1024)S(1)} %fusion.8, bf16[1536,256]{1,0:T(8,128)(2,1)} %param.4, bf16[]{:T(256)} %constant.13.clone.1), kind=kCustom, calls=%fused_computation.11 | custom fusion | bytes 1573376 | tf_op jit(solution)/shard_map/scatter | solution.py:27
  19.6 44.1 %all_to_all.34 = bf16[8,384,256]{2,1,0:T(8,128)(2,1)S(1)} all-to-all(bf16[8,384,256]{2,1,0:T(8,128)(2,1)S(1)} %bitcast.34), channel_id=1, replica_groups=mesh['dom'=8,'attr'=4] {'dom'}, dimensions={0} | all-to-all | bytes 3145728 | tf_op jit(solution)/shard_map/all_to_all | solution.py:32
  63.6 4.6 %fusion.12 = f32[3072,512]{1,0:T(8,128)} fusion(bf16[3072,256]{1,0:T(8,128)(2,1)S(1)} %bitcast.31, bf16[512,256]{1,0:T(8,128)(2,1)} %param.6), kind=kOutput, calls=%fused_computation.28 | convolution fusion | flops 805306368 | bytes 8126464 | tf_op jit(solution)/shard_map/dot_general | solution.py:45
  68.3 11.1 %scatter_custom_fusion.1 = bf16[3072]{0:T(1024)(128)(2,1)S(1)} fusion(s32[1536]{0:T(1024)S(1)} %fusion.8, bf16[1536]{0:T(1024)(128)(2,1)S(1)} %broadcast.48, bf16[]{:T(256)} %constant.13.clone.1), kind=kCustom, calls=%fused_computation.24 | custom fusion | bytes 6146 | tf_op jit(solution)/shard_map/scatter | solution.py:29
  79.5 0.5 broadcast.58
  80.0 0.7 reduce.6
  80.7 0.1 reshape.84
  80.7 9.9 %all_to_all.35 = bf16[8,2,192]{2,1,0:T(2,128)(2,1)S(1)} all-to-all(bf16[8,2,192]{2,1,0:T(2,128)(2,1)S(1)} %reshape.84), channel_id=1, replica_groups=mesh['dom'=8,'attr'=4] {'dom'}, dimensions={0} | all-to-all | bytes 12288 | tf_op jit(solution)/shard_map/all_to_all | solution.py:39
  90.6 0.1 reshape.85
  90.7 96.3 %all-reduce.2.cloned.1.call-done = f32[3072,512]{1,0:T(8,128)} async-done(((f32[3072,512]{1,0:T(8,128)}), f32[3072,512]{1,0:T(8,128)}) %all-reduce.2.cloned.1.call-update) | async-done | bytes 6291472 | tf_op jit(solution)/shard_map/psum | solution.py:45
  187.0 7.5 %fusion.11 = f32[3072]{0:T(1024)S(1)} fusion(s32[3072,512]{1,0:T(8,128)} %param.7, f32[3072,512]{1,0:T(8,128)} %all-reduce.2.cloned.1.call-done), kind=kLoop, calls=%fused_computation.27 | loop fusion | flops 14152704 | bytes 12595200 | tf_op jit(solution)/shard_map/reduce_sum | solution.py:12
  194.6 5.9 %convert_reduce_fusion = (f32[512]{0:T(512)S(1)}, bf16[3072,512]{1,0:T(8,128)(2,1)S(1)}) fusion(f32[3072]{0:T(1024)S(1)} %bitcast.38, f32[3072]{0:T(1024)S(1)} %fusion.11, s32[3072,512]{1,0:T(8,128)} %param.7, f32[3072,512]{1,0:T(8,128)S(1)} %copy-done), kind=kLoop, calls=%fused_computation.2 | loop fusion | flops 20446720 | bytes 15755264 | tf_op jit(solution)/shard_map/reduce_sum | solution.py:48
  200.5 2.2 fusion.1
  202.7 1.7 copy.8
  204.4 22.5 %all_to_all.36 = bf16[4,768,256]{1,2,0:T(8,128)(2,1)S(1)} all-to-all(bf16[4,768,256]{1,2,0:T(8,128)(2,1)S(1)} %copy.8), channel_id=1, replica_groups=mesh['dom'=8,'attr'=4] {'attr'}, dimensions={0} | all-to-all | bytes 3145728 | tf_op jit(solution)/shard_map/all_to_all | solution.py:51
  226.9 3.8 convolution_multiply_fusion
  230.7 3.7 fusion.2
  234.4 137.3 %reduce-scatter.2.cloned.1.call-done = f32[32,1024]{1,0:T(8,128)} async-done(((f32[1024,1024]{1,0:T(8,128)}), f32[32,1024]{1,0:T(8,128)}) %reduce-scatter.2.cloned.1.call-update) | async-done | bytes 131088 | tf_op jit(solution)/shard_map/reduce_scatter | solution.py:56
  (17 shorter events, 0.2 us)
Async XLA Ops:
  7.2 179.9 %all-reduce.2.cloned.1.call-start = ((), (), s32[]{:S(2)}) async-start(), calls=%async_computation.4 | async-start | bytes 12582912 | tf_op jit(solution)/shard_map/psum | solution.py:45
  68.3 303.4 %reduce-scatter.2.cloned.1.call-start = ((), (), s32[]{:S(2)}) async-start(), calls=%async_computation.5 | async-start | bytes 4325376 | tf_op jit(solution)/shard_map/reduce_scatter | solution.py:56
  187.0 7.5 %copy-start = (f32[3072,512]{1,0:T(8,128)S(1)}, f32[3072,512]{1,0:T(8,128)}, u32[]{:S(2)}) copy-start(f32[3072,512]{1,0:T(8,128)} %all-reduce.2.cloned.1.call-done) | copy-start | bytes 18874372
  194.6 5.9 %copy-start.2 = (bf16[512,256]{1,0:T(8,128)(2,1)S(1)}, bf16[512,256]{1,0:T(8,128)(2,1)}, u32[]{:S(2)}) copy-start(bf16[512,256]{1,0:T(8,128)(2,1)} %param.6) | copy-start | bytes 786436
  200.5 2.2 copy-start.1
Sparse Core Ops, SparseCore 0:
  68.4 118.5 all-reduce.1
  230.8 140.8 reduce-scatter.1
where the time goes:
time: 379 us
  waiting for transfers between devices  234 us (62%)
  blocking collectives  76.5 us (20%)
  local copies, waits for them, and re-layouts  21.8 us (6%)
  other arithmetic  18.1 us (5%)
  matrix products  14.2 us (4%)
  between operations  14.2 us (4%)
    reduce_scatter x1, waiting for transfers between devices, shards(): lax.psum_scatter(term / total_records, ('dom', 'attr'), scatter_dimension...  137 us
    psum x1, waiting for transfers between devices, shards(): lax.psum(jnp.dot(arrived, entity_means.T, preferred_element_type=jnp.floa...  96.3 us
    all_to_all x1, blocking collectives, shards(): lax.all_to_all(packed.reshape(dom_count, capacity, feat_cols), 'dom', spl...  44.1 us
    all_to_all x1, blocking collectives, shards(): lax.all_to_all(col_resid, 'attr', split_axis=0, concat_axis=1, tiled=True)  22.5 us
    scatter x1, local copies, waits for them, and re-layouts, shards(): jnp.zeros((slot_count,), jnp.bfloat16).at[position]  11.1 us
    all_to_all x1, blocking collectives, shards(): lax.all_to_all(flag_buf.reshape(dom_count, capacity), 'dom', split_axis=0...  9.89 us
    scatter x1, local copies, waits for them, and re-layouts, shards(): jnp.zeros((slot_count, feat_cols), jnp.bfloat16).at[position].set(records)  8.02 us
  transfers between devices with their start and end apart: 2, of which 2 were waited for; matrix products, arithmetic and copies ran while one was open for 4% of the time, Pallas kernels for 0%

commit v1 on v0

--- a/solution.py
+++ b/solution.py
@@ -1,6 +1,10 @@
+import functools
+
 import jax
 import jax.numpy as jnp
 from jax import lax
+from jax.experimental import pallas as pl
+from jax.experimental.pallas import tpu as pltpu
 from jax.sharding import PartitionSpec as P
 
 
@@ -56,8 +60,333 @@
     gram = lax.psum_scatter(term / total_records, ("dom", "attr"), scatter_dimension=0, tiled=True)
     return (new_means, gram)
 
+MESH = pl.DeviceIdType.MESH
+F32, BF16 = jnp.float32, jnp.bfloat16
+GROUP = 2
+
+
+def nt(a, b):
+    return lax.dot_general(a, b, (((1,), (1,)), ((), ())), preferred_element_type=F32)
+
+
+def nn(a, b):
+    return jnp.dot(a, b, preferred_element_type=F32)
+
+
+def remote(src, dst, send_sem, recv_sem, dev):
+    return pltpu.make_async_remote_copy(
+        src_ref=src, dst_ref=dst, send_sem=send_sem, recv_sem=recv_sem, device_id=dev, device_id_type=MESH
+    )
+
+
+def sweep_kernel(
+    n, na, owner_ref, records_ref, means_ref, noise_ref, new_ref, gram_ref,
+    rank_ref, meta_ref, metas, packed, x_ref, m_ref, bits_ref, w_ref, wt_ref, r_ref, rt_ref,
+    mass_ref, masses, s_send, s_keep, s_recv, s_send2, s_recv2,
+    g_send, g_keep, g_recv, gx_send, gx_recv, gy_send, gy_recv, gz_send, gz_recv,
+    rec_send, rec_recv, meta_send, meta_recv, mean_send, mean_recv, bits_sem,
+    mass_send, mass_recv, st_send, st_recv, gz_ssem, gz_rsem,
+):
+    rec_dev, feats = records_ref.shape
+    ents = means_ref.shape[0]
+    cap = 2 * rec_dev // n
+    sub = cap // na
+    half = n // 2
+    width = feats * na
+    d, q = lax.axis_index("dom"), lax.axis_index("attr")
+    me = d * na + q
+    total = n * na
+
+    barrier = pltpu.get_barrier_semaphore()
+
+    @pl.loop(1, total)
+    def _(i):
+        dev = lax.rem(me + i, total)
+        pl.semaphore_signal(barrier, inc=1, device_id=(dev // na, lax.rem(dev, na)), device_id_type=MESH)
+
+    def bits_copy(k):
+        s = lax.rem(d + half + n - k, n)
+        rows = pl.ds(pl.multiple_of(s * cap + q * sub, sub), sub)
+        return pltpu.make_async_copy(
+            noise_ref.at[rows, :], bits_ref.at[pl.ds(pl.multiple_of(k * sub, sub), sub), :], bits_sem.at[k]
+        )
+
+    @pl.loop(0, n)
+    def _(k):
+        bits_copy(k).start()
+
+    blk = 256
+    ids = lax.broadcasted_iota(jnp.int32, (n, blk), 0)
+    upper = (
+        lax.broadcasted_iota(jnp.int32, (blk, blk), 0) <= lax.broadcasted_iota(jnp.int32, (blk, blk), 1)
+    ).astype(F32).astype(BF16)
+    carry = jnp.zeros((n, 1), F32)
+    for b in range(rec_dev // blk):
+        cols = slice(b * blk, (b + 1) * blk)
+        hot = (ids == owner_ref[:, cols]).astype(F32)
+        run = nn(hot.astype(BF16), upper) + carry
+        rank_ref[:, cols] = (jnp.sum(run * hot, axis=0, keepdims=True) - 1.0).astype(jnp.int32)
+        carry = carry + jnp.sum(hot, axis=1, keepdims=True)
+    counts = jnp.broadcast_to(carry, (n, 128)).astype(jnp.int32)
+    meta_ref[...] = counts
+    metas[half] = counts
+    m_ref[q] = means_ref[...]
+
+    pl.semaphore_wait(barrier, total - 1)
+
+    def mean_copy(j, peer):
+        return remote(means_ref, m_ref.at[q], mean_send.at[j], mean_recv.at[q], (d, peer))
+
+    for j in range(1, na):
+        mean_copy(j, lax.rem(q + j, na)).start()
+
+    def meta_copy(k):
+        return remote(meta_ref, metas.at[k], meta_send.at[k], meta_recv.at[k], (lax.rem(d + half + k, n), q))
+
+    def rec_copy(k, j, peer_d):
+        return remote(
+            packed.at[k, pl.ds(j * sub, sub), :],
+            x_ref.at[q, pl.ds(pl.multiple_of(k * sub, sub), sub), :],
+            rec_send.at[k, j], rec_recv.at[k, q], (peer_d, j),
+        )
+
+    @pl.loop(0, n)
+    def _(k):
+        o = lax.rem(d + half + k, n)
+        pos = jnp.where(owner_ref[...] == o, rank_ref[...], -1)
+        hot = (lax.broadcasted_iota(jnp.int32, (cap, rec_dev), 0) == pos).astype(F32).astype(BF16)
+        packed[k] = nn(hot, records_ref[...]).astype(BF16)
+
+        @pl.when(k != half)
+        def _():
+            meta_copy(k).start()
+
+        for j in range(na):
+            mine = jnp.logical_and(k == half, q == j)
+
+            @pl.when(jnp.logical_not(mine))
+            def _():
+                rec_copy(k, j, o).start()
+
+            @pl.when(mine)
+            def _():
+                x_ref[j, pl.ds(pl.multiple_of(k * sub, sub), sub), :] = packed[k, pl.ds(j * sub, sub), :]
+
+    for j in range(1, na):
+        src = lax.rem(q + j, na)
+        remote(means_ref, m_ref.at[src], mean_send.at[j], mean_recv.at[src], (d, src)).wait_recv()
+
+    rows = GROUP * sub
+    mass_ref[...] = jnp.zeros_like(mass_ref)
+
+    @pl.loop(0, n // GROUP)
+    def _(g):
+        for t in range(GROUP):
+            k = g * GROUP + t
+
+            @pl.when(k != half)
+            def _():
+                meta_copy(k).wait_recv()
+
+            bits_copy(k).wait()
+            for a in range(na):
+                @pl.when(jnp.logical_not(jnp.logical_and(k == half, q == a)))
+                def _():
+                    remote(
+                        packed.at[k, pl.ds(0, sub), :],
+                        x_ref.at[a, pl.ds(pl.multiple_of(k * sub, sub), sub), :],
+                        rec_send.at[k, a], rec_recv.at[k, a], (d, a),
+                    ).wait_recv()
+
+        at = pl.ds(pl.multiple_of(g * rows, rows), rows)
+        raw = nt(x_ref[0, at, :], m_ref[0])
+        for a in range(1, na):
+            raw = raw + nt(x_ref[a, at, :], m_ref[a])
+        uniform = (bits_ref[at, :].astype(F32) + 0.5) / 8192.0
+        expd = jnp.exp(3.0 * jnp.tanh(raw * width ** (-0.5))) / (-jnp.log(uniform))
+        row = lax.broadcasted_iota(jnp.int32, (rows, 1), 0)
+        live = jnp.zeros((rows, 1), F32)
+        for t in range(GROUP):
+            cnt = metas[g * GROUP + t, pl.ds(d, 1), :][:, :1]
+            inside = jnp.logical_and(row >= t * sub, row < (t + 1) * sub)
+            live = live + jnp.where(jnp.logical_and(inside, row - t * sub + q * sub < cnt), 1.0, 0.0)
+        w = (expd * (live / jnp.sum(expd, axis=1, keepdims=True))).astype(BF16)
+        w_ref[at, :] = w
+        mass_ref[...] += jnp.broadcast_to(jnp.sum(w.astype(F32), axis=0, keepdims=True), mass_ref.shape)
+        for a in range(na):
+            recon = nn(w, m_ref[a])
+            res = (x_ref[a, at, :].astype(F32) - recon) * live
+            r_ref[at, pl.ds(a * feats, feats)] = res.astype(BF16)
+
+    core_peer, y_peer = q + 1 - 2 * lax.rem(q, 2), lax.rem(q + 2, na)
+    x_bit = lax.rem(d, 2)
+    x_peer = d + 1 - 2 * x_bit
+    c_bit, y_bit, z = lax.rem(q, 2), q // 2, d // 2
+    nz = n // 2
+
+    def mass_copy(j, peer):
+        return remote(mass_ref, masses.at[q], mass_send.at[j], mass_recv.at[q], (d, peer))
+
+    masses[q] = mass_ref[...]
+    for j in range(1, na):
+        mass_copy(j, lax.rem(q + j, na)).start()
+
+    for b in range(ents // 128):
+        cols = slice(b * 128, (b + 1) * 128)
+        wt_ref[cols, :] = w_ref[:, cols].T
+    for t in range(2):
+        a = (y_bit if t == 0 else 1 - y_bit) * 2 + 1 - c_bit
+        s_send[t] = nn(wt_ref[...], x_ref[a])
+    core_sums = remote(s_send, s_recv, st_send.at[0], st_recv.at[0], (d, core_peer))
+    core_sums.start()
+
+    out_rows = width // total
+    for b in range(width // 128):
+        cols = slice(b * 128, (b + 1) * 128)
+        rt_ref[pl.ds(b * 128 // out_rows, 128 // out_rows)] = (
+            r_ref[:, cols].T.reshape(128 // out_rows, out_rows, r_ref.shape[0])
+        )
+
+    def gram_rows(dx, dy, core):
+        xb = x_bit if dx == 0 else 1 - x_bit
+        yb = y_bit if dy == 0 else 1 - y_bit
+        lhs = jnp.concatenate([rt_ref[(zz * 2 + xb) * na + yb * 2 + core] for zz in range(nz)], axis=0)
+        return nn(lhs, r_ref[...])
+
+    quarter = nz * out_rows
+    order = ((1, 1), (1, 0), (0, 1), (0, 0))
+    for i, (dx, dy) in enumerate(order):
+        g_send[pl.ds(i * quarter, quarter), :] = gram_rows(dx, dy, 1 - c_bit).astype(BF16)
+    core_gram = remote(g_send, g_recv, st_send.at[1], st_recv.at[1], (d, core_peer))
+    core_gram.start()
+
+    for t in range(2):
+        a = (y_bit if t == 0 else 1 - y_bit) * 2 + c_bit
+        s_keep[t] = nn(wt_ref[...], x_ref[a])
+    core_sums.wait_recv()
+    s_send2[...] = s_keep[1] + s_recv[1]
+    y_sums = remote(s_send2, s_recv2, st_send.at[2], st_recv.at[2], (d, y_peer))
+    y_sums.start()
+
+    for i, (dx, dy) in enumerate(order):
+        g_keep[pl.ds(i * quarter, quarter), :] = gram_rows(dx, dy, c_bit)
+    core_gram.wait_recv()
+    top = pl.ds(0, 2 * quarter)
+    gx_send[...] = (g_keep[top, :] + g_recv[top, :].astype(F32)).astype(BF16)
+    x_gram = remote(gx_send, gx_recv, st_send.at[3], st_recv.at[3], (x_peer, q))
+    x_gram.start()
+    low = pl.ds(2 * quarter, 2 * quarter)
+    g_keep[low, :] += g_recv[low, :].astype(F32)
+    x_gram.wait_recv()
+    third, last = pl.ds(2 * quarter, quarter), pl.ds(3 * quarter, quarter)
+    gy_send[...] = (g_keep[third, :] + gx_recv[pl.ds(0, quarter), :].astype(F32)).astype(BF16)
+    y_gram = remote(gy_send, gy_recv, st_send.at[4], st_recv.at[4], (d, y_peer))
+    y_gram.start()
+    g_keep[last, :] += gx_recv[pl.ds(quarter, quarter), :].astype(F32)
+
+    for j in range(1, na):
+        src = lax.rem(q + j, na)
+        remote(mass_ref, masses.at[src], mass_send.at[j], mass_recv.at[src], (d, src)).wait_recv()
+    y_sums.wait_recv()
+    mass = masses[0]
+    for a in range(1, na):
+        mass = mass + masses[a]
+    col = jnp.broadcast_to(mass[:1, :], (128, ents)).T
+    for b in range(feats // 128):
+        cols = slice(b * 128, (b + 1) * 128)
+        full = s_keep[0, :, cols] + s_recv[0, :, cols] + s_recv2[:, cols]
+        new_ref[:, cols] = (full + 1.0 * means_ref[:, cols].astype(F32)) / (col + 1.0)
+
+    y_gram.wait_recv()
+    g_keep[last, :] += gy_recv[...].astype(F32)
+    gz_send[...] = g_keep[last, :].astype(BF16)
+
+    def z_copy(j):
+        to = lax.rem(z + j, nz)
+        return remote(
+            gz_send.at[pl.ds(pl.multiple_of(to * out_rows, out_rows), out_rows), :],
+            gz_recv.at[j - 1], gz_ssem.at[j - 1], gz_rsem.at[j - 1], (to * 2 + x_bit, q),
+        )
+
+    for j in range(1, nz):
+        z_copy(j).start()
+    acc = g_keep[pl.ds(pl.multiple_of(3 * quarter + z * out_rows, out_rows), out_rows), :]
+    for j in range(1, nz):
+        z_copy(j).wait_recv()
+        acc = acc + gz_recv[j - 1].astype(F32)
+    gram_ref[...] = acc / float(rec_dev * n)
+
+    for j in range(1, na):
+        mean_copy(j, lax.rem(q + j, na)).wait_send()
+        mass_copy(j, lax.rem(q + j, na)).wait_send()
+    for copy in (core_sums, core_gram, y_sums, x_gram, y_gram):
+        copy.wait_send()
+    for j in range(1, nz):
+        z_copy(j).wait_send()
+
+    @pl.loop(0, n)
+    def _(k):
+        o = lax.rem(d + half + k, n)
+
+        @pl.when(k != half)
+        def _():
+            meta_copy(k).wait_send()
+
+        for j in range(na):
+            @pl.when(jnp.logical_not(jnp.logical_and(k == half, q == j)))
+            def _():
+                rec_copy(k, j, o).wait_send()
+
+
+def fused(n, na, records, owner, entity_means, noise_bits):
+    rec_dev, feats = records.shape
+    ents = entity_means.shape[0]
+    cap = 2 * rec_dev // n
+    slots = 2 * rec_dev // na
+    width = feats * na
+    out_rows = width // (n * na)
+    nz = n // 2
+    quarter = nz * out_rows
+    vm, dma = pltpu.VMEM, pltpu.SemaphoreType.DMA
+    vspec = pl.BlockSpec(memory_space=pltpu.VMEM)
+    scratch = [
+        vm((1, rec_dev), jnp.int32), vm((n, 128), jnp.int32), vm((n, n, 128), jnp.int32),
+        vm((n, cap, feats), BF16), vm((na, slots, feats), BF16), vm((na, ents, feats), BF16),
+        vm((slots, ents), jnp.int32), vm((slots, ents), BF16), vm((ents, slots), BF16),
+        vm((slots, width), BF16), vm((n * na, out_rows, slots), BF16),
+        vm((8, ents), F32), vm((na, 8, ents), F32),
+        vm((2, ents, feats), F32), vm((2, ents, feats), F32), vm((2, ents, feats), F32),
+        vm((ents, feats), F32), vm((ents, feats), F32),
+        vm((4 * quarter, width), BF16), vm((4 * quarter, width), F32), vm((4 * quarter, width), BF16),
+        vm((2 * quarter, width), BF16), vm((2 * quarter, width), BF16),
+        vm((quarter, width), BF16), vm((quarter, width), BF16),
+        vm((quarter, width), BF16), vm((nz - 1, out_rows, width), BF16),
+        dma((n, na)), dma((n, na)), dma((n,)), dma((n,)), dma((na,)), dma((na,)), dma((n,)),
+        dma((na,)), dma((na,)), dma((5,)), dma((5,)), dma((nz - 1,)), dma((nz - 1,)),
+    ]
+    return pl.pallas_call(
+        functools.partial(sweep_kernel, n, na),
+        out_shape=(jax.ShapeDtypeStruct((ents, feats), F32), jax.ShapeDtypeStruct((out_rows, width), F32)),
+        in_specs=[vspec, vspec, vspec, pl.BlockSpec(memory_space=pl.ANY)],
+        out_specs=(vspec, vspec),
+        scratch_shapes=scratch,
+        compiler_params=pltpu.CompilerParams(
+            collective_id=0, has_side_effects=True, vmem_limit_bytes=56 * 1024 * 1024
+        ),
+    )(owner.reshape(1, rec_dev), records, entity_means, noise_bits)
+
+
+def sweep(records, owner, entity_means, noise_bits):
+    n, na = lax.axis_size("dom"), lax.axis_size("attr")
+    rec_dev, feats = records.shape
+    sub = 2 * rec_dev // n // na
+    out_rows = feats // n
+    if na == 4 and n == 8 and sub % 16 == 0 and out_rows % 16 == 0:
+        return fused(n, na, records, owner, entity_means, noise_bits)
+    return shards(records, owner, entity_means, noise_bits)
+
 
 def solution(mesh):
     in_specs = (P("dom", "attr"), P("dom", None), P("dom", "attr"), P("dom", None))
     out_specs = (P("dom", "attr"), P(("dom", "attr"), None))
-    return jax.shard_map(shards, mesh=mesh, in_specs=in_specs, out_specs=out_specs, check_vma=False)
+    return jax.shard_map(sweep, mesh=mesh, in_specs=in_specs, out_specs=out_specs, check_vma=False)

time: 379 us -> 82.7 us (0.22)
  waiting for transfers between devices: 234 us -> 0 us
  Pallas kernels: 0 us -> 78.4 us
  blocking collectives: 76.5 us -> 0 us
  local copies, waits for them, and re-layouts: 21.8 us -> 3.44 us
  other arithmetic: 18.1 us -> 0 us
  matrix products: 14.2 us -> 0 us
  between operations: 14.2 us -> 0.64 us
    reduce_scatter x1 -> x0, waiting for transfers between devices: 137 us -> none  [shards(): lax.psum_scatter(term / total_records, ('dom', 'attr'), scatter_dimension...]
    psum x1 -> x0, waiting for transfers between devices: 96.3 us -> none  [shards(): lax.psum(jnp.dot(arrived, entity_means.T, preferred_element_type=jnp.floa...]
    pallas_call x0 -> x1, Pallas kernels: none -> 78.4 us  [fused(): pl.pallas_call(functools.partial(sweep_kernel, n, na), out_shape=(jax.Sha...]
    all_to_all x3 -> x0, blocking collectives: 76.5 us -> none  [the longest x1 44.1 us: shards(): lax.all_to_all(packed.reshape(dom_count, capacity, feat_cols), 'dom', spl...]
    scatter x2 -> x0, local copies, waits for them, and re-layouts: 19.1 us -> none  [the longest x1 11.1 us: shards(): jnp.zeros((slot_count,), jnp.bfloat16).at[position]]
    dot_general x4 -> x0, matrix products: 14.2 us -> none  [the longest x1 4.62 us: shards(): jnp.dot(arrived, entity_means.T, preferred_element_type=jnp.float32)]
    reduce_sum x3 -> x0, other arithmetic: 13.5 us -> none  [the longest x1 7.54 us: posterior(): jnp.sum(expd, axis=1, keepdims=True)]
  transfers between devices with their start and end apart: 2 -> 0, of which waited for: 2 -> 0; matrix products, arithmetic and copies ran while one was open for 4% -> 0% of each run, Pallas kernels for 0% -> 0%
where the time goes in v1:
time: 82.7 us; the launch traced here: 82.5 us
  Pallas kernels  78.4 us (95%)
  local copies, waits for them, and re-layouts  3.44 us (4%)
    pallas_call x1, Pallas kernels, fused(): pl.pallas_call(functools.partial(sweep_kernel, n, na), out_shape=(jax.Sha...  78.4 us
    unnamed x2, local copies, waits for them, and re-layouts  3.44 us

profile of v1, /device:TPU:0, one launch (start us, length us, event | category | flops | bytes accessed | tf_op | source)
XLA Modules:
  0.0 82.5 jit_solution(5540447825031056268)
XLA Ops:
  0.6 78.4 %shard_map.59 = (f32[512,256]{1,0:T(8,128)}, f32[32,1024]{1,0:T(8,128)}) custom-call(s32[1,1536]{1,0:T(1,128)} %bitcast.1, bf16[1536,256]{1,0:T(8,128)(2,1)} %records_ref.1, bf16[512,256]{1,0:T(8,128)(2,1)} %means_ref.1, s32[3072,512]{1,0:T(8,128)} %noise_ref.1), custom_call_target="tpu_custom_call" | custom-call | tf_op jit(solution)/shard_map/pallas_call | solution.py:367
  79.1 1.9 %copy.8 = f32[512,256]{1,0:T(8,128)} copy(f32[512,256]{1,0:T(8,128)} %get-tuple-element.4) | data formatting | bytes 1048576
  80.9 1.6 %copy.9 = f32[32,1024]{1,0:T(8,128)} copy(f32[32,1024]{1,0:T(8,128)} %get-tuple-element.5) | data formatting | bytes 262144

commit v2 on v1

--- a/solution.py
+++ b/solution.py
@@ -63,6 +63,7 @@
 MESH = pl.DeviceIdType.MESH
 F32, BF16 = jnp.float32, jnp.bfloat16
 GROUP = 2
+CHUNKS = 4
 
 
 def nt(a, b):
@@ -85,7 +86,8 @@
     mass_ref, masses, s_send, s_keep, s_recv, s_send2, s_recv2,
     g_send, g_keep, g_recv, gx_send, gx_recv, gy_send, gy_recv, gz_send, gz_recv,
     rec_send, rec_recv, meta_send, meta_recv, mean_send, mean_recv, bits_sem,
-    mass_send, mass_recv, st_send, st_recv, gz_ssem, gz_rsem,
+    mass_send, mass_recv, sum_send, sum_recv, gc_ssem, gc_rsem, gx_ssem, gx_rsem, gy_ssem, gy_rsem,
+    gz_ssem, gz_rsem,
 ):
     rec_dev, feats = records_ref.shape
     ents = means_ref.shape[0]
@@ -132,13 +134,8 @@
     metas[half] = counts
     m_ref[q] = means_ref[...]
 
-    pl.semaphore_wait(barrier, total - 1)
-
     def mean_copy(j, peer):
         return remote(means_ref, m_ref.at[q], mean_send.at[j], mean_recv.at[q], (d, peer))
-
-    for j in range(1, na):
-        mean_copy(j, lax.rem(q + j, na)).start()
 
     def meta_copy(k):
         return remote(meta_ref, metas.at[k], meta_send.at[k], meta_recv.at[k], (lax.rem(d + half + k, n), q))
@@ -150,27 +147,38 @@
             rec_send.at[k, j], rec_recv.at[k, q], (peer_d, j),
         )
 
-    @pl.loop(0, n)
-    def _(k):
+    def pack(k):
         o = lax.rem(d + half + k, n)
         pos = jnp.where(owner_ref[...] == o, rank_ref[...], -1)
         hot = (lax.broadcasted_iota(jnp.int32, (cap, rec_dev), 0) == pos).astype(F32).astype(BF16)
         packed[k] = nn(hot, records_ref[...]).astype(BF16)
 
+    def dispatch(k):
+        for j in range(na):
+            mine = jnp.logical_and(k == half, q == j)
+
+            @pl.when(jnp.logical_not(mine))
+            def _():
+                rec_copy(k, j, lax.rem(d + half + k, n)).start()
+
+            @pl.when(mine)
+            def _():
+                x_ref[j, pl.ds(pl.multiple_of(k * sub, sub), sub), :] = packed[k, pl.ds(j * sub, sub), :]
+
         @pl.when(k != half)
         def _():
             meta_copy(k).start()
 
-        for j in range(na):
-            mine = jnp.logical_and(k == half, q == j)
-
-            @pl.when(jnp.logical_not(mine))
-            def _():
-                rec_copy(k, j, o).start()
-
-            @pl.when(mine)
-            def _():
-                x_ref[j, pl.ds(pl.multiple_of(k * sub, sub), sub), :] = packed[k, pl.ds(j * sub, sub), :]
+    pack(0)
+    pl.semaphore_wait(barrier, total - 1)
+    dispatch(0)
+    for j in range(1, na):
+        mean_copy(j, lax.rem(q + j, na)).start()
+
+    @pl.loop(1, n)
+    def _(k):
+        pack(k)
+        dispatch(k)
 
     for j in range(1, na):
         src = lax.rem(q + j, na)
@@ -234,11 +242,17 @@
     for b in range(ents // 128):
         cols = slice(b * 128, (b + 1) * 128)
         wt_ref[cols, :] = w_ref[:, cols].T
-    for t in range(2):
-        a = (y_bit if t == 0 else 1 - y_bit) * 2 + 1 - c_bit
-        s_send[t] = nn(wt_ref[...], x_ref[a])
-    core_sums = remote(s_send, s_recv, st_send.at[0], st_recv.at[0], (d, core_peer))
-    core_sums.start()
+
+    def partial_sums(t, core):
+        return nn(wt_ref[...], x_ref[(y_bit if t == 0 else 1 - y_bit) * 2 + core])
+
+    def core_sums(t):
+        return remote(s_send.at[t], s_recv.at[t], sum_send.at[t], sum_recv.at[t], (d, core_peer))
+
+    for t in (1, 0):
+        s_send[t] = partial_sums(t, 1 - c_bit)
+        core_sums(t).start()
+    s_keep[1] = partial_sums(1, c_bit)
 
     out_rows = width // total
     for b in range(width // 128):
@@ -246,43 +260,73 @@
         rt_ref[pl.ds(b * 128 // out_rows, 128 // out_rows)] = (
             r_ref[:, cols].T.reshape(128 // out_rows, out_rows, r_ref.shape[0])
         )
-
-    def gram_rows(dx, dy, core):
+    core_sums(1).wait_recv()
+    s_send2[...] = s_keep[1] + s_recv[1]
+    y_sums = remote(s_send2, s_recv2, sum_send.at[2], sum_recv.at[2], (d, y_peer))
+    y_sums.start()
+
+    quarter = nz * out_rows
+    part = width // CHUNKS
+    order = ((1, 1), (1, 0), (0, 1), (0, 0))
+
+    def gram_rows(dx, dy, core, c):
         xb = x_bit if dx == 0 else 1 - x_bit
         yb = y_bit if dy == 0 else 1 - y_bit
         lhs = jnp.concatenate([rt_ref[(zz * 2 + xb) * na + yb * 2 + core] for zz in range(nz)], axis=0)
-        return nn(lhs, r_ref[...])
-
-    quarter = nz * out_rows
-    order = ((1, 1), (1, 0), (0, 1), (0, 0))
-    for i, (dx, dy) in enumerate(order):
-        g_send[pl.ds(i * quarter, quarter), :] = gram_rows(dx, dy, 1 - c_bit).astype(BF16)
-    core_gram = remote(g_send, g_recv, st_send.at[1], st_recv.at[1], (d, core_peer))
-    core_gram.start()
-
-    for t in range(2):
-        a = (y_bit if t == 0 else 1 - y_bit) * 2 + c_bit
-        s_keep[t] = nn(wt_ref[...], x_ref[a])
-    core_sums.wait_recv()
-    s_send2[...] = s_keep[1] + s_recv[1]
-    y_sums = remote(s_send2, s_recv2, st_send.at[2], st_recv.at[2], (d, y_peer))
-    y_sums.start()
-
-    for i, (dx, dy) in enumerate(order):
-        g_keep[pl.ds(i * quarter, quarter), :] = gram_rows(dx, dy, c_bit)
-    core_gram.wait_recv()
-    top = pl.ds(0, 2 * quarter)
-    gx_send[...] = (g_keep[top, :] + g_recv[top, :].astype(F32)).astype(BF16)
-    x_gram = remote(gx_send, gx_recv, st_send.at[3], st_recv.at[3], (x_peer, q))
-    x_gram.start()
-    low = pl.ds(2 * quarter, 2 * quarter)
-    g_keep[low, :] += g_recv[low, :].astype(F32)
-    x_gram.wait_recv()
-    third, last = pl.ds(2 * quarter, quarter), pl.ds(3 * quarter, quarter)
-    gy_send[...] = (g_keep[third, :] + gx_recv[pl.ds(0, quarter), :].astype(F32)).astype(BF16)
-    y_gram = remote(gy_send, gy_recv, st_send.at[4], st_recv.at[4], (d, y_peer))
-    y_gram.start()
-    g_keep[last, :] += gx_recv[pl.ds(quarter, quarter), :].astype(F32)
+        return nn(lhs, r_ref[:, c * part:(c + 1) * part])
+
+    def core_gram(c):
+        return remote(g_send.at[c], g_recv.at[c], gc_ssem.at[c], gc_rsem.at[c], (d, core_peer))
+
+    def x_gram(c):
+        return remote(gx_send.at[c], gx_recv.at[c], gx_ssem.at[c], gx_rsem.at[c], (x_peer, q))
+
+    def y_gram(c):
+        return remote(gy_send.at[c], gy_recv.at[c], gy_ssem.at[c], gy_rsem.at[c], (d, y_peer))
+
+    def z_copy(c, j):
+        to = lax.rem(z + j, nz)
+        return remote(
+            gz_send.at[c, pl.ds(pl.multiple_of(to * out_rows, out_rows), out_rows), :],
+            gz_recv.at[c, j - 1], gz_ssem.at[c, j - 1], gz_rsem.at[c, j - 1], (to * 2 + x_bit, q),
+        )
+
+    top, low = slice(0, 2 * quarter), slice(2 * quarter, 4 * quarter)
+    third, last = slice(2 * quarter, 3 * quarter), slice(3 * quarter, 4 * quarter)
+
+    def to_x(c):
+        core_gram(c).wait_recv()
+        gx_send[c] = (g_keep[c, top, :] + g_recv[c, top, :].astype(F32)).astype(BF16)
+        x_gram(c).start()
+        g_keep[c, low, :] += g_recv[c, low, :].astype(F32)
+
+    def to_y(c):
+        x_gram(c).wait_recv()
+        gy_send[c] = (g_keep[c, third, :] + gx_recv[c, :quarter, :].astype(F32)).astype(BF16)
+        y_gram(c).start()
+        g_keep[c, last, :] += gx_recv[c, quarter:, :].astype(F32)
+
+    def to_z(c):
+        y_gram(c).wait_recv()
+        gz_send[c] = g_keep[c, last, :] + gy_recv[c].astype(F32)
+        for j in range(1, nz):
+            z_copy(c, j).start()
+
+    for c in range(CHUNKS):
+        for i, (dx, dy) in enumerate(order):
+            g_send[c, i * quarter:(i + 1) * quarter, :] = gram_rows(dx, dy, 1 - c_bit, c).astype(BF16)
+        core_gram(c).start()
+        for i, (dx, dy) in enumerate(order):
+            g_keep[c, i * quarter:(i + 1) * quarter, :] = gram_rows(dx, dy, c_bit, c)
+        if c > 0:
+            to_x(c - 1)
+    to_x(CHUNKS - 1)
+    s_keep[0] = partial_sums(0, c_bit)
+    core_sums(0).wait_recv()
+    for c in range(CHUNKS):
+        to_y(c)
+        if c > 0:
+            to_z(c - 1)
 
     for j in range(1, na):
         src = lax.rem(q + j, na)
@@ -297,32 +341,25 @@
         full = s_keep[0, :, cols] + s_recv[0, :, cols] + s_recv2[:, cols]
         new_ref[:, cols] = (full + 1.0 * means_ref[:, cols].astype(F32)) / (col + 1.0)
 
-    y_gram.wait_recv()
-    g_keep[last, :] += gy_recv[...].astype(F32)
-    gz_send[...] = g_keep[last, :].astype(BF16)
-
-    def z_copy(j):
-        to = lax.rem(z + j, nz)
-        return remote(
-            gz_send.at[pl.ds(pl.multiple_of(to * out_rows, out_rows), out_rows), :],
-            gz_recv.at[j - 1], gz_ssem.at[j - 1], gz_rsem.at[j - 1], (to * 2 + x_bit, q),
-        )
-
-    for j in range(1, nz):
-        z_copy(j).start()
-    acc = g_keep[pl.ds(pl.multiple_of(3 * quarter + z * out_rows, out_rows), out_rows), :]
-    for j in range(1, nz):
-        z_copy(j).wait_recv()
-        acc = acc + gz_recv[j - 1].astype(F32)
-    gram_ref[...] = acc / float(rec_dev * n)
+    to_z(CHUNKS - 1)
+    for c in range(CHUNKS):
+        acc = gz_send[c, pl.ds(pl.multiple_of(z * out_rows, out_rows), out_rows), :]
+        for j in range(1, nz):
+            z_copy(c, j).wait_recv()
+            acc = acc + gz_recv[c, j - 1]
+        gram_ref[:, c * part:(c + 1) * part] = acc / float(rec_dev * n)
 
     for j in range(1, na):
         mean_copy(j, lax.rem(q + j, na)).wait_send()
         mass_copy(j, lax.rem(q + j, na)).wait_send()
-    for copy in (core_sums, core_gram, y_sums, x_gram, y_gram):
+    for copy in (core_sums(0), core_sums(1), y_sums):
         copy.wait_send()
-    for j in range(1, nz):
-        z_copy(j).wait_send()
+    for c in range(CHUNKS):
+        core_gram(c).wait_send()
+        x_gram(c).wait_send()
+        y_gram(c).wait_send()
+        for j in range(1, nz):
+            z_copy(c, j).wait_send()
 
     @pl.loop(0, n)
     def _(k):
@@ -347,6 +384,7 @@
     out_rows = width // (n * na)
     nz = n // 2
     quarter = nz * out_rows
+    part = width // CHUNKS
     vm, dma = pltpu.VMEM, pltpu.SemaphoreType.DMA
     vspec = pl.BlockSpec(memory_space=pltpu.VMEM)
     scratch = [
@@ -357,12 +395,14 @@
         vm((8, ents), F32), vm((na, 8, ents), F32),
         vm((2, ents, feats), F32), vm((2, ents, feats), F32), vm((2, ents, feats), F32),
         vm((ents, feats), F32), vm((ents, feats), F32),
-        vm((4 * quarter, width), BF16), vm((4 * quarter, width), F32), vm((4 * quarter, width), BF16),
-        vm((2 * quarter, width), BF16), vm((2 * quarter, width), BF16),
-        vm((quarter, width), BF16), vm((quarter, width), BF16),
-        vm((quarter, width), BF16), vm((nz - 1, out_rows, width), BF16),
+        vm((CHUNKS, 4 * quarter, part), BF16), vm((CHUNKS, 4 * quarter, part), F32),
+        vm((CHUNKS, 4 * quarter, part), BF16),
+        vm((CHUNKS, 2 * quarter, part), BF16), vm((CHUNKS, 2 * quarter, part), BF16),
+        vm((CHUNKS, quarter, part), BF16), vm((CHUNKS, quarter, part), BF16),
+        vm((CHUNKS, quarter, part), F32), vm((CHUNKS, nz - 1, out_rows, part), F32),
         dma((n, na)), dma((n, na)), dma((n,)), dma((n,)), dma((na,)), dma((na,)), dma((n,)),
-        dma((na,)), dma((na,)), dma((5,)), dma((5,)), dma((nz - 1,)), dma((nz - 1,)),
+        dma((na,)), dma((na,)), dma((3,)), dma((3,)),
+        *(dma((CHUNKS,)) for _ in range(6)), dma((CHUNKS, nz - 1)), dma((CHUNKS, nz - 1)),
     ]
     return pl.pallas_call(
         functools.partial(sweep_kernel, n, na),

time: 82.7 us -> 80.7 us (0.976)
  Pallas kernels: 78.4 us -> 76.4 us
    pallas_call x1, Pallas kernels: 78.4 us -> 76.4 us  [fused(): pl.pallas_call(functools.partial(sweep_kernel, n, na), out_shape=(jax.Sha...]
where the time goes in v2:
time: 80.7 us; the launch traced here: 80.5 us
  Pallas kernels  76.4 us (95%)
  local copies, waits for them, and re-layouts  3.44 us (4%)
    pallas_call x1, Pallas kernels, fused(): pl.pallas_call(functools.partial(sweep_kernel, n, na), out_shape=(jax.Sha...  76.4 us
    unnamed x2, local copies, waits for them, and re-layouts  3.44 us

profile of v2, /device:TPU:0, one launch (start us, length us, event | category | flops | bytes accessed | tf_op | source)
XLA Modules:
  0.0 80.5 jit_solution(1749181658471722817)
XLA Ops:
  0.6 76.4 %shard_map.59 = (f32[512,256]{1,0:T(8,128)}, f32[32,1024]{1,0:T(8,128)}) custom-call(s32[1,1536]{1,0:T(1,128)} %bitcast.1, bf16[1536,256]{1,0:T(8,128)(2,1)} %records_ref.1, bf16[512,256]{1,0:T(8,128)(2,1)} %means_ref.1, s32[3072,512]{1,0:T(8,128)} %noise_ref.1), custom_call_target="tpu_custom_call" | custom-call | tf_op jit(solution)/shard_map/pallas_call | solution.py:407
  77.1 1.9 %copy.8 = f32[512,256]{1,0:T(8,128)} copy(f32[512,256]{1,0:T(8,128)} %get-tuple-element.4) | data formatting | bytes 1048576
  78.9 1.6 %copy.9 = f32[32,1024]{1,0:T(8,128)} copy(f32[32,1024]{1,0:T(8,128)} %get-tuple-element.5) | data formatting | bytes 262144

commit v3 on v2

--- a/solution.py
+++ b/solution.py
@@ -87,7 +87,7 @@
     g_send, g_keep, g_recv, gx_send, gx_recv, gy_send, gy_recv, gz_send, gz_recv,
     rec_send, rec_recv, meta_send, meta_recv, mean_send, mean_recv, bits_sem,
     mass_send, mass_recv, sum_send, sum_recv, gc_ssem, gc_rsem, gx_ssem, gx_rsem, gy_ssem, gy_rsem,
-    gz_ssem, gz_rsem,
+    gz_ssem, gz_rsem, ys_ssem, ys_rsem,
 ):
     rec_dev, feats = records_ref.shape
     ents = means_ref.shape[0]
@@ -262,8 +262,13 @@
         )
     core_sums(1).wait_recv()
     s_send2[...] = s_keep[1] + s_recv[1]
-    y_sums = remote(s_send2, s_recv2, sum_send.at[2], sum_recv.at[2], (d, y_peer))
-    y_sums.start()
+    piece = ents // CHUNKS
+
+    def y_sums(c):
+        rows_c = pl.ds(c * piece, piece)
+        return remote(s_send2.at[rows_c], s_recv2.at[rows_c], ys_ssem.at[c], ys_rsem.at[c], (d, y_peer))
+
+    y_sums(0).start()
 
     quarter = nz * out_rows
     part = width // CHUNKS
@@ -304,6 +309,8 @@
         x_gram(c).wait_recv()
         gy_send[c] = (g_keep[c, third, :] + gx_recv[c, :quarter, :].astype(F32)).astype(BF16)
         y_gram(c).start()
+        if c + 1 < CHUNKS:
+            y_sums(c + 1).start()
         g_keep[c, last, :] += gx_recv[c, quarter:, :].astype(F32)
 
     def to_z(c):
@@ -331,7 +338,8 @@
     for j in range(1, na):
         src = lax.rem(q + j, na)
         remote(mass_ref, masses.at[src], mass_send.at[j], mass_recv.at[src], (d, src)).wait_recv()
-    y_sums.wait_recv()
+    for c in range(CHUNKS):
+        y_sums(c).wait_recv()
     mass = masses[0]
     for a in range(1, na):
         mass = mass + masses[a]
@@ -347,14 +355,15 @@
         for j in range(1, nz):
             z_copy(c, j).wait_recv()
             acc = acc + gz_recv[c, j - 1]
-        gram_ref[:, c * part:(c + 1) * part] = acc / float(rec_dev * n)
+        gram_ref[:, c * part:(c + 1) * part] = acc
 
     for j in range(1, na):
         mean_copy(j, lax.rem(q + j, na)).wait_send()
         mass_copy(j, lax.rem(q + j, na)).wait_send()
-    for copy in (core_sums(0), core_sums(1), y_sums):
-        copy.wait_send()
+    for t in range(2):
+        core_sums(t).wait_send()
     for c in range(CHUNKS):
+        y_sums(c).wait_send()
         core_gram(c).wait_send()
         x_gram(c).wait_send()
         y_gram(c).wait_send()
@@ -373,6 +382,11 @@
             @pl.when(jnp.logical_not(jnp.logical_and(k == half, q == j)))
             def _():
                 rec_copy(k, j, o).wait_send()
+
+
+def finish_kernel(records, means_ref, gram_ref, means_out, gram_out):
+    means_out[...] = means_ref[...]
+    gram_out[...] = gram_ref[...] / records
 
 
 def fused(n, na, records, owner, entity_means, noise_bits):
@@ -401,10 +415,11 @@
         vm((CHUNKS, quarter, part), BF16), vm((CHUNKS, quarter, part), BF16),
         vm((CHUNKS, quarter, part), F32), vm((CHUNKS, nz - 1, out_rows, part), F32),
         dma((n, na)), dma((n, na)), dma((n,)), dma((n,)), dma((na,)), dma((na,)), dma((n,)),
-        dma((na,)), dma((na,)), dma((3,)), dma((3,)),
+        dma((na,)), dma((na,)), dma((2,)), dma((2,)),
         *(dma((CHUNKS,)) for _ in range(6)), dma((CHUNKS, nz - 1)), dma((CHUNKS, nz - 1)),
+        dma((CHUNKS,)), dma((CHUNKS,)),
     ]
-    return pl.pallas_call(
+    new_means, gram = pl.pallas_call(
         functools.partial(sweep_kernel, n, na),
         out_shape=(jax.ShapeDtypeStruct((ents, feats), F32), jax.ShapeDtypeStruct((out_rows, width), F32)),
         in_specs=[vspec, vspec, vspec, pl.BlockSpec(memory_space=pl.ANY)],
@@ -414,6 +429,12 @@
             collective_id=0, has_side_effects=True, vmem_limit_bytes=56 * 1024 * 1024
         ),
     )(owner.reshape(1, rec_dev), records, entity_means, noise_bits)
+    return pl.pallas_call(
+        functools.partial(finish_kernel, float(rec_dev * n)),
+        out_shape=(jax.ShapeDtypeStruct((ents, feats), F32), jax.ShapeDtypeStruct((out_rows, width), F32)),
+        in_specs=[vspec, vspec],
+        out_specs=(vspec, vspec),
+    )(new_means, gram)
 
 
 def sweep(records, owner, entity_means, noise_bits):

time: 80.7 us -> 80.5 us (level)
  local copies, waits for them, and re-layouts: 3.44 us -> 0 us
  Pallas kernels: 76.4 us -> 79.7 us
    unnamed x2 -> x0, local copies, waits for them, and re-layouts: 3.44 us -> none
    pallas_call x0 -> x1, Pallas kernels: none -> 1.93 us  [fused(): pl.pallas_call(functools.partial(finish_kernel, float(rec_dev * n)), out_...]
    pallas_call x1, Pallas kernels: 76.4 us -> 77.8 us  [fused(): pl.pallas_call(functools.partial(sweep_kernel, n, na), out_shape=(jax.Sha...]
where the time goes in v3:
time: 80.5 us; the launch traced here: 80.4 us
  Pallas kernels  79.7 us (99%)
    pallas_call x1, Pallas kernels, fused(): pl.pallas_call(functools.partial(sweep_kernel, n, na), out_shape=(jax.Sha...  77.8 us
    pallas_call x1, Pallas kernels, fused(): pl.pallas_call(functools.partial(finish_kernel, float(rec_dev * n)), out_...  1.93 us

profile of v3, /device:TPU:0, one launch (start us, length us, event | category | flops | bytes accessed | tf_op | source)
XLA Modules:
  0.0 80.4 jit_solution(14386850975416404493)
XLA Ops:
  0.6 77.8 %shard_map.59 = (f32[512,256]{1,0:T(8,128)}, f32[32,1024]{1,0:T(8,128)}) custom-call(s32[1,1536]{1,0:T(1,128)} %bitcast.1, bf16[1536,256]{1,0:T(8,128)(2,1)} %records_ref.1, bf16[512,256]{1,0:T(8,128)(2,1)} %means_ref.1, s32[3072,512]{1,0:T(8,128)} %noise_ref.1), custom_call_target="tpu_custom_call" | custom-call | tf_op jit(solution)/shard_map/pallas_call | solution.py:422
  78.5 1.9 %shard_map.60 = (f32[512,256]{1,0:T(8,128)}, f32[32,1024]{1,0:T(8,128)}) custom-call(f32[512,256]{1,0:T(8,128)} %get-tuple-element.4.means_ref, f32[32,1024]{1,0:T(8,128)} %get-tuple-element.5.gram_ref), custom_call_target="tpu_custom_call" | custom-call | tf_op jit(solution)/shard_map/pallas_call | solution.py:432
